TPU v7x, 32 devices: a whole 2x2x4 slice. The times are simulated.
32 devices in a mesh: row: 4 (over z), col: 4 (over y, core), depth: 2 (over x).
Axes of the slice: x: 2, y: 2, z: 4, core: 2. Of those that a mesh axis runs over, the one named last changes fastest.
Arguments:
- tokens: bfloat16 [256, 12288], P(('row', 'col'), 'depth'), may hold values from -6 to 6
- in_weight: bfloat16 [12288, 49152], P('depth', ('row', 'col')), may hold values from -0.0546875 to 0.0546875
- in_bias: bfloat16 [49152], P(('row', 'col')), may hold values from -4 to 4
- out_weight: bfloat16 [49152, 12288], P(('row', 'col'), 'depth'), may hold values from -0.02734375 to 0.02734375
- out_bias: bfloat16 [12288], P('depth'), may hold values from -3 to 3
Outputs:
- outputs: bfloat16 [256, 12288], P(('row', 'col'), 'depth')
All inputs are finite; a program needn't handle non-finite values.
Results may differ from a plain program's by a relative error of at most 0.0045.
Values may be sent and summed in bfloat16 or wider, within the bound.
A program may use at most 192 MiB of HBM per device.

v0:
```python
import jax
import jax.numpy as jnp
from jax import lax
from jax.sharding import PartitionSpec as P


def body(tokens, in_weight, in_bias, out_weight, out_bias):
    partial_value = jnp.dot(
        lax.all_gather(tokens, ("row", "col"), axis=0, tiled=True),
        in_weight,
        preferred_element_type=jnp.float32,
    )
    bias_row = in_bias.astype(jnp.float32)
    summed = lax.psum(partial_value, "depth")
    hidden = jax.nn.gelu(summed + bias_row, approximate=True).astype(jnp.bfloat16)
    outputs = lax.psum_scatter(
        jnp.dot(hidden, out_weight, preferred_element_type=jnp.float32),
        ("row", "col"),
        scatter_dimension=0,
        tiled=True,
    )
    return (outputs + out_bias.astype(jnp.float32)).astype(jnp.bfloat16)


def solution(mesh):
    in_specs = (
        P(("row", "col"), "depth"),
        P("depth", ("row", "col")),
        P(("row", "col")),
        P(("row", "col"), "depth"),
        P("depth"),
    )
    out_specs = P(("row", "col"), "depth")
    return jax.shard_map(body, mesh=mesh, in_specs=in_specs, out_specs=out_specs, check_vma=False)
```

profile of v0, /device:TPU:0, one launch (start us, length us, event | category | flops | bytes accessed | tf_op | source)
XLA Modules:
  0.0 274.8 jit_solution(7004497836152599166)
XLA Ops:
  6.5 0.0 all-gather.2.cloned.1.call-start
  6.5 0.7 all-gather.2.cloned.1.call-update
  7.3 0.0 all-reduce.2.cloned.1.call-start
  7.3 50.3 %all-gather.2.cloned.1.call-done = bf16[256,6144]{1,0:T(8,128)(2,1)} async-done(((bf16[16,6144]{1,0:T(8,128)(2,1)}), bf16[256,6144]{1,0:T(8,128)(2,1)}) %all-gather.2.cloned.1.call-update) | async-done | bytes 3145744 | tf_op jit(solution)/shard_map/all_gather | solution.py:9
  57.6 18.8 %fusion.19 = f32[256,3072]{1,0:T(8,128)} fusion(bf16[256,6144]{1,0:T(8,128)(2,1)} %all-gather.2.cloned.1.call-done, bf16[6144,3072]{1,0:T(8,128)(2,1)} %param.6), kind=kOutput, calls=%fused_computation.20 | convolution fusion | flops 9663676416 | bytes 44040192 | tf_op jit(solution)/shard_map/dot_general | solution.py:8
  76.4 0.0 copy-start.1
  76.4 0.0 all-reduce.2.cloned.1.call-update
  76.4 0.0 reduce-scatter.2.cloned.1.call-start
  76.5 0.6 copy-done.1
  77.1 84.1 %all-reduce.2.cloned.1.call-done = f32[256,3072]{1,0:T(8,128)} async-done(((f32[256,3072]{1,0:T(8,128)}), f32[256,3072]{1,0:T(8,128)}) %all-reduce.2.cloned.1.call-update) | async-done | bytes 3145744 | tf_op jit(solution)/shard_map/psum | solution.py:14
  161.1 19.9 %fusion.8 = f32[256,6144]{1,0:T(8,128)} fusion(bf16[3072,6144]{1,0:T(8,128)(2,1)} %param.8, f32[256,3072]{1,0:T(8,128)} %all-reduce.2.cloned.1.call-done, f32[3072]{0:T(1024)S(1)} %convert_element_type.12), kind=kOutput, calls=%fused_computation.9 | convolution fusion | flops 9671540736 | bytes 47198208 | tf_op jit(solution)/shard_map/dot_general | solution.py:17
  181.1 0.0 copy-start
  181.1 0.0 reduce-scatter.2.cloned.1.call-update
  181.1 0.7 copy-done
  181.8 84.7 %reduce-scatter.2.cloned.1.call-done = f32[16,6144]{1,0:T(8,128)} async-done(((f32[256,6144]{1,0:T(8,128)}), f32[16,6144]{1,0:T(8,128)}) %reduce-scatter.2.cloned.1.call-update) | async-done | bytes 393232 | tf_op jit(solution)/shard_map/reduce_scatter | solution.py:16
  266.5 1.7 add_convert_fusion
  (2 shorter events, 0.0 us)
Async XLA Ops:
  6.5 51.0 %all-gather.2.cloned.1.call-start = ((), (), s32[]{:S(2)}) async-start(), calls=%async_computation.1 | async-start | bytes 3342336 | tf_op jit(solution)/shard_map/all_gather | solution.py:9
  7.3 153.9 %all-reduce.2.cloned.1.call-start = ((), (), s32[]{:S(2)}) async-start(), calls=%async_computation.2 | async-start | bytes 6291456 | tf_op jit(solution)/shard_map/psum | solution.py:14
  76.4 0.7 copy-start.1
  76.4 190.1 %reduce-scatter.2.cloned.1.call-start = ((), (), s32[]{:S(2)}) async-start(), calls=%async_computation.3 | async-start | bytes 6684672 | tf_op jit(solution)/shard_map/reduce_scatter | solution.py:16
  181.1 0.7 copy-start
Sparse Core Ops, SparseCore 0:
  9.6 47.8 all-gather.1
  76.5 84.5 all-reduce.1
  181.2 85.2 reduce-scatter.1
where the time goes:
time: 275 us
  waiting for transfers between devices  220 us (80%)
  matrix products  38.8 us (14%)
  between operations  13.1 us (5%)
    reduce_scatter x1, waiting for transfers between devices, body(): lax.psum_scatter(jnp.dot(hidden, out_weight, preferred_element_type=jnp.f...  84.7 us
    psum x1, waiting for transfers between devices, body(): summed = lax.psum(partial_value, 'depth')  84.1 us
    all_gather x1, waiting for transfers between devices, body(): lax.all_gather(tokens, ('row', 'col'), axis=0, tiled=True)  50.3 us
    dot_general x1, matrix products, body(): jnp.dot(hidden, out_weight, preferred_element_type=jnp.float32)  19.9 us
    dot_general x1, matrix products, body(): jnp.dot(lax.all_gather(tokens, ('row', 'col'), axis=0, tiled=True), in_we...  18.8 us
  transfers between devices with their start and end apart: 3, of which 3 were waited for; matrix products, arithmetic and copies ran while one was open for 0% of the time, Pallas kernels for 0%

commit v1 on v0

--- a/solution.py
+++ b/solution.py
@@ -4,11 +4,21 @@
 from jax.sharding import PartitionSpec as P
 
 
+def gather_by_bits(x, axis, dim):
+    ways, here, hop = (lax.axis_size(axis), lax.axis_index(axis), x.shape[dim])
+    line, have = (x, 1)
+    while have < ways:
+        line = jnp.concatenate(
+            [line, lax.ppermute(line, axis, [(d, (d - have) % ways) for d in range(ways)])],
+            axis=dim,
+        )
+        have = 2 * have
+    return jnp.roll(line, here * hop, axis=dim)
+
+
 def body(tokens, in_weight, in_bias, out_weight, out_bias):
     partial_value = jnp.dot(
-        lax.all_gather(tokens, ("row", "col"), axis=0, tiled=True),
-        in_weight,
-        preferred_element_type=jnp.float32,
+        gather_by_bits(tokens, ("row", "col"), 0), in_weight, preferred_element_type=jnp.float32
     )
     bias_row = in_bias.astype(jnp.float32)
     summed = lax.psum(partial_value, "depth")

time: 275 us -> 342 us (1.24)
  waiting for transfers between devices: 220 us -> 266 us
  local copies, waits for them, and re-layouts: 1.3 us -> 11 us
  starting transfers between devices: 0.08 us -> 8.02 us
    ppermute x0 -> x4, waiting for transfers between devices: none -> 97.5 us  [gather_by_bits(): lax.ppermute(line, axis, [(d, (d - have) % ways) for d in range(ways)])]
    all_gather x1 -> x0, waiting for transfers between devices: 50.3 us -> none  [body(): lax.all_gather(tokens, ('row', 'col'), axis=0, tiled=True)]
    unnamed x4 -> x15, local copies, waits for them, and re-layouts: 1.3 us -> 9.67 us
    ppermute x0 -> x4, starting transfers between devices: none -> 7.97 us  [gather_by_bits(): lax.ppermute(line, axis, [(d, (d - have) % ways) for d in range(ways)])]
  transfers between devices with their start and end apart: 3 -> 6, of which waited for: 3 -> 6; matrix products, arithmetic and copies ran while one was open for 0% -> 1% of each run, Pallas kernels for 0% -> 0%
where the time goes in v1:
time: 342 us
  waiting for transfers between devices  266 us (78%)
  matrix products  38.8 us (11%)
  between operations  13.4 us (4%)
  local copies, waits for them, and re-layouts  11 us (3%)
  starting transfers between devices  8.02 us (2%)
  other arithmetic  4.68 us (1%)
    ppermute x4, waiting for transfers between devices, gather_by_bits(): lax.ppermute(line, axis, [(d, (d - have) % ways) for d in range(ways)])  97.5 us
    reduce_scatter x1, waiting for transfers between devices, body(): lax.psum_scatter(jnp.dot(hidden, out_weight, preferred_element_type=jnp.f...  84.7 us
    psum x1, waiting for transfers between devices, body(): summed = lax.psum(partial_value, 'depth')  83.5 us
    dot_general x1, matrix products, body(): jnp.dot(hidden, out_weight, preferred_element_type=jnp.float32)  20 us
    dot_general x1, matrix products, body(): jnp.dot(gather_by_bits(tokens, ('row', 'col'), 0), in_weight, preferred_e...  18.8 us
    unnamed x15, local copies, waits for them, and re-layouts  9.67 us
    ppermute x4, starting transfers between devices, gather_by_bits(): lax.ppermute(line, axis, [(d, (d - have) % ways) for d in range(ways)])  7.97 us
  transfers between devices with their start and end apart: 6, of which 6 were waited for; matrix products, arithmetic and copies ran while one was open for 1% of the time, Pallas kernels for 0%

profile of v1, /device:TPU:0, one launch (start us, length us, event | category | flops | bytes accessed | tf_op | source)
XLA Modules:
  0.0 341.6 jit_solution(5993452394209728028)
XLA Ops:
  6.5 5.4 %collective-permute-start = (bf16[16,6144]{1,0:T(8,128)(2,1)}, bf16[16,6144]{1,0:T(8,128)(2,1)S(1)}, u32[]{:S(2)}, u32[]{:S(2)}) collective-permute-start(bf16[16,6144]{1,0:T(8,128)(2,1)} %param.5), channel_id=1, source_target_pairs={{0,30},{2,0},{4,2},{6,4},{8,6},{10,8},{12,10},{14,12},{16,14},{18,... | collective-permute-start | bytes 589832 | tf_op jit(solution)/shard_map/ppermute | solution.py:12
  12.0 3.5 %collective-permute-done = bf16[16,6144]{1,0:T(8,128)(2,1)S(1)} collective-permute-done((bf16[16,6144]{1,0:T(8,128)(2,1)}, bf16[16,6144]{1,0:T(8,128)(2,1)S(1)}, u32[]{:S(2)}, u32[]{:S(2)}) %collective-permute-start) | collective-permute-done | bytes 196640 | tf_op jit(solution)/shard_map/ppermute | solution.py:12
  15.5 1.0 pad_maximum_fusion.2
  16.4 0.6 collective-permute-start.1
  17.1 8.8 %collective-permute-done.1 = bf16[32,6144]{1,0:T(8,128)(2,1)S(1)} collective-permute-done((bf16[32,6144]{1,0:T(8,128)(2,1)S(1)}, bf16[32,6144]{1,0:T(8,128)(2,1)S(1)}, u32[]{:S(2)}, u32[]{:S(2)}) %collective-permute-start.1) | collective-permute-done | bytes 393248 | tf_op jit(solution)/shard_map/ppermute | solution.py:12
  25.8 1.0 pad_maximum_fusion.1
  26.8 0.8 collective-permute-start.2
  27.6 1.6 constant_dynamic-update-slice_fusion.9
  29.2 17.9 %collective-permute-done.2 = bf16[64,6144]{1,0:T(8,128)(2,1)S(1)} collective-permute-done((bf16[64,6144]{1,0:T(8,128)(2,1)S(1)}, bf16[64,6144]{1,0:T(8,128)(2,1)S(1)}, u32[]{:S(2)}, u32[]{:S(2)}) %collective-permute-start.2) | collective-permute-done | bytes 786464 | tf_op jit(solution)/shard_map/ppermute | solution.py:12
  47.2 1.0 pad_maximum_fusion
  48.2 0.0 copy-start
  48.2 1.1 collective-permute-start.3
  49.3 0.7 constant_dynamic-update-slice_fusion.8
  50.0 0.8 constant_dynamic-update-slice_fusion.7
  50.8 1.0 constant_dynamic-update-slice_fusion.6
  51.8 67.3 %collective-permute-done.3 = bf16[128,6144]{1,0:T(8,128)(2,1)S(1)} collective-permute-done((bf16[128,6144]{1,0:T(8,128)(2,1)S(1)}, bf16[128,6144]{1,0:T(8,128)(2,1)S(1)}, u32[]{:S(2)}, u32[]{:S(2)}) %collective-permute-start.3) | collective-permute-done | bytes 1572896 | tf_op jit(solution)/shard_map/ppermute | solution.py:12
  119.0 1.3 constant_dynamic-update-slice_fusion.5
  120.3 0.7 constant_dynamic-update-slice_fusion.4
  121.0 0.7 constant_dynamic-update-slice_fusion.3
  121.6 0.8 constant_dynamic-update-slice_fusion.2
  122.4 0.9 constant_dynamic-update-slice_fusion.1
  123.4 1.3 constant_dynamic-update-slice_fusion
  124.6 18.8 %fusion.8 = f32[256,3072]{1,0:T(8,128)} fusion(bf16[6144,3072]{1,0:T(8,128)(2,1)} %param.6, bf16[512,6144]{1,0:T(8,128)(2,1)} %constant_dynamic-update-slice_fusion, s32[]{:T(128)S(6)} %select_n.14), kind=kOutput, calls=%fused_computation.9 | convolution fusion | flops 9663676416 | bytes 44040196 | tf_op jit(solution)/shard_map/dot_general | solution.py:20
  143.5 0.0 all-reduce.2.cloned.1.call-update
  143.5 0.0 reduce-scatter.2.cloned.1.call-start
  143.5 0.6 copy-done.2
  144.2 83.5 %all-reduce.2.cloned.1.call-done = f32[256,3072]{1,0:T(8,128)} async-done(((f32[256,3072]{1,0:T(8,128)}), f32[256,3072]{1,0:T(8,128)}) %all-reduce.2.cloned.1.call-update) | async-done | bytes 3145744 | tf_op jit(solution)/shard_map/psum | solution.py:24
  227.7 20.0 %fusion.10 = f32[256,6144]{1,0:T(8,128)} fusion(bf16[3072,6144]{1,0:T(8,128)(2,1)} %param.8, f32[256,3072]{1,0:T(8,128)} %all-reduce.2.cloned.1.call-done, f32[3072]{0:T(1024)S(1)} %convert_element_type.12), kind=kOutput, calls=%fused_computation.11 | convolution fusion | flops 9671540736 | bytes 47198208 | tf_op jit(solution)/shard_map/dot_general | solution.py:27
  247.7 0.0 reduce-scatter.2.cloned.1.call-update
  247.7 0.7 copy-done.1
  248.4 84.7 %reduce-scatter.2.cloned.1.call-done = f32[16,6144]{1,0:T(8,128)} async-done(((f32[256,6144]{1,0:T(8,128)}), f32[16,6144]{1,0:T(8,128)}) %reduce-scatter.2.cloned.1.call-update) | async-done | bytes 393232 | tf_op jit(solution)/shard_map/reduce_scatter | solution.py:26
  333.1 1.7 add_convert_fusion
  (6 shorter events, 0.0 us)
Async XLA Ops:
  6.5 221.1 %all-reduce.2.cloned.1.call-start = ((), (), s32[]{:S(2)}) async-start(), calls=%async_computation.1 | async-start | bytes 6291456 | tf_op jit(solution)/shard_map/psum | solution.py:24
  6.5 8.9 %collective-permute-start = (bf16[16,6144]{1,0:T(8,128)(2,1)}, bf16[16,6144]{1,0:T(8,128)(2,1)S(1)}, u32[]{:S(2)}, u32[]{:S(2)}) collective-permute-start(bf16[16,6144]{1,0:T(8,128)(2,1)} %param.5), channel_id=1, source_target_pairs={{0,30},{2,0},{4,2},{6,4},{8,6},{10,8},{12,10},{14,12},{16,14},{18,... | collective-permute-start | bytes 589832 | tf_op jit(solution)/shard_map/ppermute | solution.py:12
  16.4 9.4 %collective-permute-start.1 = (bf16[32,6144]{1,0:T(8,128)(2,1)S(1)}, bf16[32,6144]{1,0:T(8,128)(2,1)S(1)}, u32[]{:S(2)}, u32[]{:S(2)}) collective-permute-start(bf16[32,6144]{1,0:T(8,128)(2,1)S(1)} %pad_maximum_fusion.2), channel_id=1, source_target_pairs={{0,28},{2,30},{4,0},{6,2},{8,4},{10,6},{12,8},{14,10},{16,12},{18,... | collective-permute-start | bytes 1179656 | tf_op jit(solution)/shard_map/ppermute | solution.py:12
  26.8 20.3 %collective-permute-start.2 = (bf16[64,6144]{1,0:T(8,128)(2,1)S(1)}, bf16[64,6144]{1,0:T(8,128)(2,1)S(1)}, u32[]{:S(2)}, u32[]{:S(2)}) collective-permute-start(bf16[64,6144]{1,0:T(8,128)(2,1)S(1)} %pad_maximum_fusion.1), channel_id=1, source_target_pairs={{0,24},{2,26},{4,28},{6,30},{8,0},{10,2},{12,4},{14,6},{16,8},{18,... | collective-permute-start | bytes 2359304 | tf_op jit(solution)/shard_map/ppermute | solution.py:12
  48.2 72.1 %copy-start = (bf16[16,6144]{1,0:T(8,128)(2,1)S(1)}, bf16[16,6144]{1,0:T(8,128)(2,1)}, u32[]{:S(2)}) copy-start(bf16[16,6144]{1,0:T(8,128)(2,1)} %param.5) | copy-start | bytes 589828
  48.2 70.8 %collective-permute-start.3 = (bf16[128,6144]{1,0:T(8,128)(2,1)S(1)}, bf16[128,6144]{1,0:T(8,128)(2,1)S(1)}, u32[]{:S(2)}, u32[]{:S(2)}) collective-permute-start(bf16[128,6144]{1,0:T(8,128)(2,1)S(1)} %pad_maximum_fusion), channel_id=1, source_target_pairs={{0,16},{2,18},{4,20},{6,22},{8,24},{10,26},{12,28},{14,30},{16,0},... | collective-permute-start | bytes 4718600 | tf_op jit(solution)/shard_map/ppermute | solution.py:12
  143.5 0.7 copy-start.2
  143.5 189.6 %reduce-scatter.2.cloned.1.call-start = ((), (), s32[]{:S(2)}) async-start(), calls=%async_computation.2 | async-start | bytes 6684672 | tf_op jit(solution)/shard_map/reduce_scatter | solution.py:26
  247.7 0.7 copy-start.1
Sparse Core Ops, SparseCore 0:
  143.6 84.0 all-reduce.1
  247.8 85.1 reduce-scatter.1
